TPU v7x, 512 devices: a whole 4x4x16 slice. The times are simulated.
512 devices in a mesh: req: 64 (over z, x), head: 8 (over y, core).
Axes of the slice: x: 4, y: 4, z: 16, core: 2. Of those that a mesh axis runs over, the one named last changes fastest.
Arguments:
- tokens: bfloat16 [64, 512, 1024], P('req', 'head'), may hold values from -6 to 6
- gain: bfloat16 [1024], replicated, may hold values from 0.099609375 to 1.8984375
- projection_weight: bfloat16 [1024, 4, 1024], P(None, None, 'head'), may hold values from -0.1875 to 0.1875
- output_weight: bfloat16 [1024, 1024], P('head'), may hold values from -0.1875 to 0.1875
- persist: bfloat16 [2, 16, 1024], P(None, None, 'head'), may hold values from -6 to 6
- cache_page_slots: bfloat16 [64, 64, 64, 2, 1024], P('req', None, None, None, 'head'), may hold values from -250 to 250
- cached_length: int32 [64], P('req'), may hold values from 33 to 4096, as said below
- page_keeper: int32 [64, 128], P('req'), may hold values from -1 to 63, as said below
- page_slot_index: int32 [64, 128], P('req'), may hold values from -1 to 1, as said below
- memory_state: float32 [2, 64, 8, 128, 128], P(None, 'req', 'head'), may hold values from -3 to 3
- retention: float32 [64, 8], P('req', 'head'), may hold values from 0.2 to 1
- momentum: float32 [64, 8], P('req', 'head'), may hold values from 0.2 to 0.9
- memory_step_scale: float32 [64, 8], P('req', 'head'), may hold values from 0.02 to 0.3
- halving_updates: int32 [64, 8], P('req'), may hold values 0 or 1
Outputs:
- layer_out: bfloat16 [64, 512, 1024], P('req', 'head')
- new_state: float32 [2, 64, 8, 128, 128], P(None, 'req', 'head')
Inputs may be any that keep to these rules, and one draw needn't show every extreme that they name: `cached_length`: the requests of one device hold together at most 128 pages. `page_keeper`: pages j below cached_length[r] / 32 (rounded up) have a keeper; later entries are -1. No keeper and slot serve two pages of the requests of one device. `page_slot_index`: -1 exactly where page_keeper is -1.
All inputs are finite; a program needn't handle non-finite values. No bound on the sum of `halving_updates` on one device may be relied on, other than what follows from the above.
Results may differ from a plain program's by a relative error of at most 0.012.
The roundings to bfloat16 on the way count: a program that leaves them out, or rounds other values in their place, can miss the bound.
Values may be sent and summed in bfloat16 or wider, within the bound.
A program may use at most 64 MiB of HBM per device.

v0:
```python
import math
import jax
import jax.numpy as jnp
from jax import lax
from jax.sharding import PartitionSpec as P

HD = 128
BLK = 64
PAGE = 32
norm_eps = 1e-05
unit_eps = 1e-06


def unit_rows(values_f):
    return values_f * lax.rsqrt(jnp.sum(values_f * values_f, axis=-1, keepdims=True) + unit_eps)


def against(left, right):
    return lax.dot_general(
        left, right, (((1,), (1,)), ((), ())), preferred_element_type=jnp.float32
    )


def exact_rows(left, right):
    return lax.dot_general(
        left,
        right,
        (((1,), (1,)), ((), ())),
        precision=lax.Precision.HIGHEST,
        preferred_element_type=jnp.float32,
    )


def exact_outer(left, right):
    return lax.dot_general(
        left,
        right,
        (((0,), (0,)), ((), ())),
        precision=lax.Precision.HIGHEST,
        preferred_element_type=jnp.float32,
    )


def shards(
    tokens,
    gain,
    projection_weight,
    output_weight,
    persist,
    cache_page_slots,
    cached_length,
    page_keeper,
    page_slot_index,
    memory_state,
    retention,
    momentum,
    memory_step_scale,
    halving_updates,
):
    req_dev = tokens.shape[0]
    width = tokens.shape[2]
    head_cols = projection_weight.shape[2]
    homes = cache_page_slots.shape[1]
    lanes = cache_page_slots.shape[2] // PAGE
    max_pages = page_keeper.shape[1]
    scale = 1.0 / math.sqrt(HD)
    gain_f = gain.astype(jnp.float32)
    flat_w = projection_weight.reshape(width, 4 * head_cols)
    piece_f = lax.all_gather(tokens, "head", axis=1, tiled=True).astype(jnp.float32)
    scaled = (
        piece_f * lax.rsqrt(jnp.mean(piece_f * piece_f, axis=-1, keepdims=True) + norm_eps) * gain_f
    )
    normed = scaled.astype(jnp.bfloat16)
    count = normed.shape[0] * normed.shape[1]
    result = jnp.dot(normed.reshape(count, width), flat_w, preferred_element_type=jnp.float32)
    projected = result.reshape(normed.shape[0], normed.shape[1], 4, head_cols)
    queries = projected[:, :, 0].astype(jnp.bfloat16)
    own_keys = projected[:, :, 1].astype(jnp.bfloat16)
    own_values = projected[:, :, 2].astype(jnp.bfloat16)
    gates = projected[:, :, 3]
    prefill = queries.shape[1]
    kept_span = lanes * PAGE
    received = lax.all_to_all(cache_page_slots, "req", split_axis=1, concat_axis=0, tiled=True)
    cache_keys = received[:, 0, :, 0, :].reshape(homes * kept_span, head_cols)
    cache_values = received[:, 0, :, 1, :].reshape(homes * kept_span, head_cols)
    page_ids = jnp.arange(max_pages, dtype=jnp.int32)
    filled = jnp.clip(cached_length[:, None] - page_ids[None, :] * PAGE, 0, PAGE)
    slot_of = page_keeper * lanes + page_slot_index
    slot_ids = jnp.arange(homes * lanes, dtype=jnp.int32)
    slot_fill = jnp.sum(
        jnp.where(slot_of[:, :, None] == slot_ids[None, None, :], filled[:, :, None], 0), axis=1
    )
    position = jnp.arange(PAGE, dtype=jnp.int32)
    full_valid = (position[None, None, :] < slot_fill[:, :, None]).reshape(
        req_dev, homes, lanes * PAGE
    )
    cache_valid = full_valid.reshape(req_dev, homes * kept_span)
    causal = jnp.arange(prefill)[:, None] >= jnp.arange(prefill)[None, :]
    upper_col = HD
    query_head = queries[0, :, 0:upper_col]
    key_head = own_keys[0, :, 0:upper_col]
    value_head = own_values[0, :, 0:upper_col]
    score_p = against(query_head, persist[0, :, 0:upper_col]) * scale
    score_c = jnp.where(cache_valid[0][None, :], against(query_head, cache_keys) * scale, -jnp.inf)
    score_t = jnp.where(causal, against(query_head, key_head) * scale, -jnp.inf)
    row_max = jnp.maximum(
        jnp.maximum(
            jnp.max(score_p, axis=-1, keepdims=True), jnp.max(score_c, axis=-1, keepdims=True)
        ),
        jnp.max(score_t, axis=-1, keepdims=True),
    )
    exp_p = jnp.exp(score_p - row_max)
    exp_c = jnp.exp(score_c - row_max)
    exp_t = jnp.exp(score_t - row_max)
    total = (
        jnp.sum(exp_p, axis=-1, keepdims=True)
        + jnp.sum(exp_c, axis=-1, keepdims=True)
        + jnp.sum(exp_t, axis=-1, keepdims=True)
    )
    mixed = jnp.dot(
        exp_p.astype(jnp.bfloat16), persist[1, :, 0:upper_col], preferred_element_type=jnp.float32
    )
    mixed = mixed + jnp.dot(
        exp_c.astype(jnp.bfloat16), cache_values, preferred_element_type=jnp.float32
    )
    mixed = mixed + jnp.dot(
        exp_t.astype(jnp.bfloat16), value_head, preferred_element_type=jnp.float32
    )
    attended = mixed / total
    unit_attn = attended * lax.rsqrt(
        jnp.mean(attended * attended, axis=-1, keepdims=True) + unit_eps
    )
    query_unit = unit_rows(query_head.astype(jnp.float32))
    key_unit = unit_rows(key_head.astype(jnp.float32))
    value_f = value_head.astype(jnp.float32)
    state_m = memory_state[0, 0, 0]
    state_s = memory_state[1, 0, 0]
    reads = []
    for block_span in range(prefill // BLK):
        lower = block_span * BLK
        q_block = query_unit[lower : lower + BLK]
        k_block = key_unit[lower : lower + BLK]
        v_block = value_f[lower : lower + BLK]
        reads.append(exact_rows(q_block, state_m))
        errors = exact_rows(k_block, state_m) - v_block
        grads = exact_outer(errors, k_block)
        state_s = momentum[0, 0] * state_s - memory_step_scale[0, 0] * grads
        keeper_list = retention[0, 0] * jnp.where(halving_updates[0, block_span] == 1, 0.5, 1.0)
        state_m = keeper_list * state_m + state_s
    memory_read = jnp.concatenate(reads, axis=0)
    head_outs = unit_attn + jax.nn.sigmoid(gates[0, :, 0:upper_col]) * memory_read
    head_states = [jnp.stack([state_m, state_s])]
    request_outs = [head_outs.astype(jnp.bfloat16)]
    state_rows = [jnp.stack(head_states, axis=1)]
    mixed_heads = jnp.stack(request_outs)
    new_state = jnp.stack(state_rows, axis=1)
    regrouped = lax.all_to_all(mixed_heads, "head", split_axis=1, concat_axis=2, tiled=True)
    row_count = regrouped.shape[1]
    piece = lax.all_gather(output_weight, "head", axis=0, tiled=True)
    groups = piece.shape[0] // head_cols
    section = regrouped
    section = section.reshape(req_dev, row_count, groups, head_cols)
    blocks = piece.reshape(groups, head_cols, width)
    sums = jnp.einsum("atgc,gcd->atgd", section, blocks, preferred_element_type=jnp.float32)
    rounded = lax.optimization_barrier(sums.astype(jnp.bfloat16))
    layer_f = jnp.sum(rounded.astype(jnp.float32), axis=2)
    return (layer_f.astype(jnp.bfloat16), new_state)


def solution(mesh):
    in_specs = (
        P("req", "head", None),
        P(),
        P(None, None, "head"),
        P("head", None),
        P(None, None, "head"),
        P("req", None, None, None, "head"),
        P("req"),
        P("req", None),
        P("req", None),
        P(None, "req", "head", None, None),
        P("req", "head"),
        P("req", "head"),
        P("req", "head"),
        P("req", None),
    )
    out_specs = (P("req", "head", None), P(None, "req", "head", None, None))
    return jax.shard_map(shards, mesh=mesh, in_specs=in_specs, out_specs=out_specs, check_vma=False)
```

profile of v0, /device:TPU:1, one launch (start us, length us, event | category | flops | bytes accessed | tf_op | source)
XLA Modules:
  0.0 161.1 jit_solution(271079519594700890)
XLA Ops:
  7.3 0.7 all-gather.3.cloned.1.call-update
  7.9 3.5 %copy.44 = bf16[1,64,64,2,128]{4,2,3,0,1:T(8,128)(2,1)} copy(bf16[1,64,64,2,128]{4,3,2,1,0:T(2,128)(2,1)} %param.19) | data formatting | bytes 4194304 | tf_op args[5]
  11.4 19.2 %all-to-all-start = ((bf16[1,64,64,2,128]{4,2,3,0,1:T(8,128)(2,1)}), bf16[1,64,64,2,128]{4,2,3,0,1:T(8,128)(2,1)S(1)}, u32[]{:S(2)}, u32[]{:S(2)}) async-start(bf16[1,64,64,2,128]{4,2,3,0,1:T(8,128)(2,1)} %copy.44), calls=%async_computation | async-start | bytes 4194304 | tf_op jit(solution)/shard_map/all_to_all | solution.py:83
  30.7 0.7 all-gather.5.cloned.1.call-update
  31.4 1.4 copy.60
  32.9 1.3 copy.43
  34.2 0.7 fusion.85
  43.0 3.8 %all-gather.3.cloned.1.call-done = bf16[1,512,1024]{2,1,0:T(8,128)(2,1)} async-done(((bf16[1,64,1024]{2,1,0:T(8,128)(2,1)}), bf16[1,512,1024]{2,1,0:T(8,128)(2,1)}) %all-gather.3.cloned.1.call-update) | async-done | bytes 1048592 | tf_op jit(solution)/shard_map/all_gather | solution.py:69
  46.8 1.5 fusion.6
  48.3 2.3 %convolution_bitcast_fusion = f32[1,512,4,128]{3,1,2,0:T(8,128)S(1)} fusion(bf16[4,128,1024]{2,1,0:T(8,128)(2,1)} %bitcast.161, bf16[1,512,1024]{2,1,0:T(8,128)(2,1)} %all-gather.3.cloned.1.call-done, f32[1024]{0:T(1024)S(1)} %convert_element_type.76, f32[512]{0:T(512)S(1)} %add_rsqrt_fusion.3), kind=kOutput, calls=%fused_computation.17 | convolution fusion | flops 538968064 | bytes 3151872 | tf_op jit(solution)/shard_map/dot_general | solution.py:75
  51.7 0.3 fusion.43
  52.5 0.3 multiply_add_fusion.5
  53.3 0.3 multiply_add_fusion.4
  54.1 0.3 multiply_add_fusion.3
  54.9 0.3 multiply_add_fusion.2
  55.7 0.3 multiply_add_fusion.1
  56.5 0.3 multiply_add_fusion
  57.5 0.3 fusion.12
  57.8 0.3 fusion.86
  58.1 67.5 %all-to-all-done = bf16[1,64,64,2,128]{4,2,3,0,1:T(8,128)(2,1)S(1)} async-done(((bf16[1,64,64,2,128]{4,2,3,0,1:T(8,128)(2,1)}), bf16[1,64,64,2,128]{4,2,3,0,1:T(8,128)(2,1)S(1)}, u32[]{:S(2)}, u32[]{:S(2)}) %all-to-all-start) | async-done | bytes 2097184 | tf_op jit(solution)/shard_map/all_to_all | solution.py:83
  126.0 1.4 fusion
  127.7 2.2 %fusion.1 = f32[512]{0:T(512)S(1)} fusion(f32[512,4096]{1,0:T(8,128)S(1)} %get-tuple-element.44, f32[512]{0:T(512)S(1)} %maximum_maximum_fusion, pred[4096]{0:T(1024)(128)(4,1)S(1)} %lt.27), kind=kLoop, calls=%fused_computation.3 | loop fusion | flops 8388096 | bytes 8396800 | tf_op jit(solution)/shard_map/reduce_sum | solution.py:117
  129.9 1.7 %fusion.3 = f32[512,128]{1,0:T(8,128)S(1)} fusion(bf16[4096,128]{1,0:T(8,128)(2,1)S(1)} %bitcast.162, f32[512,4096]{1,0:T(8,128)S(1)} %get-tuple-element.44, f32[512]{0:T(512)S(1)} %maximum_maximum_fusion, pred[4096]{0:T(1024)(128)(4,1)S(1)} %lt.27), kind=kOutput, calls=%fused_computation.5 | convolution fusion | flops 545259520 | bytes 9705472 | tf_op jit(solution)/shard_map/dot_general | solution.py:123
  131.9 0.5 multiply_reduce_fusion
  132.7 0.5 broadcast.141
  133.2 1.4 reduce.4
  134.7 0.7 reshape.270
  135.3 10.6 %all-to-all-start.1 = ((bf16[8,2,4096]{2,1,0:T(2,128)(2,1)}), bf16[8,2,4096]{2,1,0:T(2,128)(2,1)S(1)}, u32[]{:S(2)}, u32[]{:S(2)}) async-start(bf16[8,2,4096]{2,1,0:T(2,128)(2,1)} %reshape.270), calls=%async_computation.1 | async-start | bytes 262144 | tf_op jit(solution)/shard_map/all_to_all | solution.py:157
  146.0 0.7 maximum_bitcast_fusion
  146.6 4.6 %all-to-all-done.1 = bf16[8,2,4096]{2,1,0:T(2,128)(2,1)S(1)} async-done(((bf16[8,2,4096]{2,1,0:T(2,128)(2,1)}), bf16[8,2,4096]{2,1,0:T(2,128)(2,1)S(1)}, u32[]{:S(2)}, u32[]{:S(2)}) %all-to-all-start.1) | async-done | bytes 131104 | tf_op jit(solution)/shard_map/all_to_all | solution.py:157
  151.4 2.0 %fusion.9 = bf16[1,64,8,1024]{3,1,2,0:T(8,128)(2,1)S(1)} fusion(bf16[64,8,128]{2,0,1:T(8,128)(2,1)S(1)} %bitcast.164, bf16[8,128,1024]{2,1,0:T(8,128)(2,1)} %bitcast.157), kind=kOutput, calls=%fused_computation.14 | convolution fusion | flops 134742016 | bytes 3276800 | tf_op jit(solution)/shard_map/atgc,gcd->atgd/dot_general | solution.py:164
  153.4 0.8 reduce_sum.94
  (69 shorter events, 6.4 us)
Async XLA Ops:
  7.2 27.0 %copy-start.7 = (bf16[1024]{0:T(1024)(128)(2,1)S(1)}, bf16[1024]{0:T(1024)(128)(2,1)}, u32[]{:S(2)}) copy-start(bf16[1024]{0:T(1024)(128)(2,1)} %param.15) | copy-start | bytes 6148
  7.2 27.0 %copy-start.5 = (s32[1,8]{1,0:T(1,128)S(1)}, s32[1,8]{1,0:T(1,128)}, u32[]{:S(2)}) copy-start(s32[1,8]{1,0:T(1,128)} %param.27) | copy-start | bytes 100
  7.2 35.4 %copy-start.9 = (s32[1,128]{1,0:T(1,128)S(1)}, s32[1,128]{1,0:T(1,128)}, u32[]{:S(2)}) copy-start(s32[1,128]{1,0:T(1,128)} %param.21) | copy-start | bytes 1540
  7.2 35.4 %copy-start.8 = (s32[1,128]{1,0:T(1,128)S(1)}, s32[1,128]{1,0:T(1,128)}, u32[]{:S(2)}) copy-start(s32[1,128]{1,0:T(1,128)} %param.22) | copy-start | bytes 1540
  7.2 39.6 %all-gather.3.cloned.1.call-start = ((), (), s32[]{:S(2)}) async-start(), calls=%async_computation.2 | async-start | bytes 1179648 | tf_op jit(solution)/shard_map/all_gather | solution.py:69
  11.4 39.8 %copy-start.4 = (f32[2,1,1,128,128]{4,3,2,1,0:T(8,128)S(1)}, f32[2,1,1,128,128]{4,3,2,1,0:T(8,128)}, u32[]{:S(2)}) copy-start(f32[2,1,1,128,128]{4,3,2,1,0:T(8,128)} %param.23) | copy-start | bytes 393220
  11.4 114.3 %all-to-all-start = ((bf16[1,64,64,2,128]{4,2,3,0,1:T(8,128)(2,1)}), bf16[1,64,64,2,128]{4,2,3,0,1:T(8,128)(2,1)S(1)}, u32[]{:S(2)}, u32[]{:S(2)}) async-start(bf16[1,64,64,2,128]{4,2,3,0,1:T(8,128)(2,1)} %copy.44), calls=%async_computation | async-start | bytes 4194304 | tf_op jit(solution)/shard_map/all_to_all | solution.py:83
  30.7 26.6 %copy-start.6 = (bf16[2,16,128]{2,1,0:T(8,128)(2,1)S(1)}, bf16[2,16,128]{2,1,0:T(8,128)(2,1)}, u32[]{:S(2)}) copy-start(bf16[2,16,128]{2,1,0:T(8,128)(2,1)} %param.18) | copy-start | bytes 24580
  30.7 120.7 %all-gather.5.cloned.1.call-start = ((), (), s32[]{:S(2)}) async-start(), calls=%async_computation.3 | async-start | bytes 2359296 | tf_op jit(solution)/shard_map/all_gather | solution.py:159
  50.6 7.2 %copy-start = (f32[1,512,4,128]{3,1,2,0:T(8,128)}, f32[1,512,4,128]{3,1,2,0:T(8,128)S(1)}, u32[]{:S(2)}) copy-start(f32[1,512,4,128]{3,1,2,0:T(8,128)S(1)} %convolution_bitcast_fusion) | copy-start | bytes 3145732
  57.0 0.7 copy-start.2
  129.9 2.0 %copy-start.1 = (f32[1,512,4,128]{3,1,2,0:T(8,128)S(1)}, f32[1,512,4,128]{3,1,2,0:T(8,128)}, u32[]{:S(2)}) copy-start(f32[1,512,4,128]{3,1,2,0:T(8,128)} %copy-done) | copy-start | bytes 3145732
  129.9 2.5 %copy-start.3 = (f32[512,128]{1,0:T(8,128)S(1)}, f32[512,128]{1,0:T(8,128)}, u32[]{:S(2)}) copy-start(f32[512,128]{1,0:T(8,128)} %copy-done.2) | copy-start | bytes 786436
  135.3 15.9 %all-to-all-start.1 = ((bf16[8,2,4096]{2,1,0:T(2,128)(2,1)}), bf16[8,2,4096]{2,1,0:T(2,128)(2,1)S(1)}, u32[]{:S(2)}, u32[]{:S(2)}) async-start(bf16[8,2,4096]{2,1,0:T(2,128)(2,1)} %reshape.270), calls=%async_computation.1 | async-start | bytes 262144 | tf_op jit(solution)/shard_map/all_to_all | solution.py:157
Sparse Core Ops, SparseCore 0:
  10.2 36.6 all-gather.2
  49.0 32.9 all-gather.4
where the time goes:
time: 162 us; the launch traced here: 161 us
  waiting for transfers between devices  77.3 us (48%)
  starting transfers between devices  29.9 us (18%)
  between operations  22.2 us (14%)
  matrix products  14.8 us (9%)
  local copies, waits for them, and re-layouts  9.12 us (6%)
  other arithmetic  7.67 us (5%)
    all_to_all x1, waiting for transfers between devices, shards(): lax.all_to_all(cache_page_slots, 'req', split_axis=1, concat_axis=0, tile...  67.5 us
    all_to_all x1, starting transfers between devices, shards(): lax.all_to_all(cache_page_slots, 'req', split_axis=1, concat_axis=0, tile...  19.2 us
    all_to_all x1, starting transfers between devices, shards(): lax.all_to_all(mixed_heads, 'head', split_axis=1, concat_axis=2, tiled=True)  10.6 us
    unnamed x26, local copies, waits for them, and re-layouts  6.3 us
    all_to_all x1, waiting for transfers between devices, shards(): lax.all_to_all(mixed_heads, 'head', split_axis=1, concat_axis=2, tiled=True)  4.58 us
    dot_general x16, matrix products, exact_rows(): lax.dot_general(left, right, (((1,), (1,)), ((), ())), precision=lax.Prec...  3.83 us
    all_gather x1, waiting for transfers between devices, shards(): lax.all_gather(tokens, 'head', axis=1, tiled=True).astype(jnp.float32)  3.79 us
  transfers between devices with their start and end apart: 4, of which 3 were waited for; matrix products, arithmetic and copies ran while one was open for 18% of the time, Pallas kernels for 0%

commit v1 on v0

--- a/solution.py
+++ b/solution.py
@@ -66,7 +66,9 @@
     scale = 1.0 / math.sqrt(HD)
     gain_f = gain.astype(jnp.float32)
     flat_w = projection_weight.reshape(width, 4 * head_cols)
-    piece_f = lax.all_gather(tokens, "head", axis=1, tiled=True).astype(jnp.float32)
+    piece_f = jnp.concatenate(
+        lax.all_to_all(jnp.stack([tokens] * lax.axis_size("head")), "head", 0, 0), axis=1
+    ).astype(jnp.float32)
     scaled = (
         piece_f * lax.rsqrt(jnp.mean(piece_f * piece_f, axis=-1, keepdims=True) + norm_eps) * gain_f
     )

time: 162 us -> 183 us (1.13)
  waiting for transfers between devices: 77.3 us -> 92 us
  starting transfers between devices: 29.9 us -> 33 us
  local copies, waits for them, and re-layouts: 9.12 us -> 12.1 us
    all_to_all x1, waiting for transfers between devices: 67.5 us -> 86.7 us  [shards(): lax.all_to_all(cache_page_slots, 'req', split_axis=1, concat_axis=0, tile...]
    all_to_all x0 -> x1, starting transfers between devices: none -> 10.3 us  [shards(): lax.all_to_all(jnp.stack([tokens] * lax.axis_size('head')), 'head', 0, 0)]
    all_to_all x1, starting transfers between devices: 19.2 us -> 14.1 us  [shards(): lax.all_to_all(cache_page_slots, 'req', split_axis=1, concat_axis=0, tile...]
    all_gather x1 -> x0, waiting for transfers between devices: 3.79 us -> none  [shards(): lax.all_gather(tokens, 'head', axis=1, tiled=True).astype(jnp.float32)]
    all_to_all x1, starting transfers between devices: 10.6 us -> 8.61 us  [shards(): lax.all_to_all(mixed_heads, 'head', split_axis=1, concat_axis=2, tiled=True)]
    another operation x0 -> x1, local copies, waits for them, and re-layouts: none -> 2.01 us  [shards(): jnp.stack([tokens] * lax.axis_size('head'))]
    unnamed x26 -> x18, local copies, waits for them, and re-layouts: 6.3 us -> 6.29 us
  transfers between devices with their start and end apart: 4 -> 4, of which waited for: 3 -> 2; matrix products, arithmetic and copies ran while one was open for 18% -> 16% of each run, Pallas kernels for 0% -> 0%
where the time goes in v1:
time: 183 us; the launch traced here: 182 us
  waiting for transfers between devices  92 us (50%)
  starting transfers between devices  33 us (18%)
  between operations  22.2 us (12%)
  matrix products  14.5 us (8%)
  local copies, waits for them, and re-layouts  12.1 us (7%)
  other arithmetic  8.12 us (4%)
    all_to_all x1, waiting for transfers between devices, shards(): lax.all_to_all(cache_page_slots, 'req', split_axis=1, concat_axis=0, tile...  86.7 us
    all_to_all x1, starting transfers between devices, shards(): lax.all_to_all(cache_page_slots, 'req', split_axis=1, concat_axis=0, tile...  14.1 us
    all_to_all x1, starting transfers between devices, shards(): lax.all_to_all(jnp.stack([tokens] * lax.axis_size('head')), 'head', 0, 0)  10.3 us
    all_to_all x1, starting transfers between devices, shards(): lax.all_to_all(mixed_heads, 'head', split_axis=1, concat_axis=2, tiled=True)  8.61 us
    unnamed x18, local copies, waits for them, and re-layouts  6.29 us
    all_to_all x1, waiting for transfers between devices, shards(): lax.all_to_all(mixed_heads, 'head', split_axis=1, concat_axis=2, tiled=True)  4.58 us
    dot_general x16, matrix products, exact_rows(): lax.dot_general(left, right, (((1,), (1,)), ((), ())), precision=lax.Prec...  3.83 us
  transfers between devices with their start and end apart: 4, of which 2 were waited for; matrix products, arithmetic and copies ran while one was open for 16% of the time, Pallas kernels for 0%

profile of v1, /device:TPU:1, one launch (start us, length us, event | category | flops | bytes accessed | tf_op | source)
XLA Modules:
  0.0 181.9 jit_solution(17519912648984389074)
XLA Ops:
  7.2 2.0 %stack.10 = bf16[8,1,64,1024]{3,2,1,0:T(8,128)(2,1)} broadcast(bf16[64,1024]{1,0:T(8,128)(2,1)} %bitcast.167), dimensions={2,3} | broadcast | bytes 1179648 | tf_op jit(solution)/shard_map/stack | solution.py:70
  9.2 10.3 %all-to-all-start = ((bf16[8,1,64,1024]{3,2,1,0:T(8,128)(2,1)}), bf16[8,1,64,1024]{3,2,1,0:T(8,128)(2,1)S(1)}, u32[]{:S(2)}, u32[]{:S(2)}) async-start(bf16[8,1,64,1024]{3,2,1,0:T(8,128)(2,1)} %stack.10), calls=%async_computation | async-start | bytes 2097152 | tf_op jit(solution)/shard_map/all_to_all | solution.py:70
  19.5 0.7 all-gather.2.cloned.1.call-update
  20.2 0.7 convert_element_type.92
  20.9 1.4 copy.60
  22.3 1.3 copy.43
  25.6 1.6 fusion.81
  33.0 0.7 add_bitcast_fusion.1
  34.0 3.5 %copy.44 = bf16[1,64,64,2,128]{4,2,3,0,1:T(8,128)(2,1)} copy(bf16[1,64,64,2,128]{4,3,2,1,0:T(2,128)(2,1)} %param.19) | data formatting | bytes 4194304 | tf_op args[5]
  37.6 14.1 %all-to-all-start.1 = ((bf16[1,64,64,2,128]{4,2,3,0,1:T(8,128)(2,1)}), bf16[1,64,64,2,128]{4,2,3,0,1:T(8,128)(2,1)S(1)}, u32[]{:S(2)}, u32[]{:S(2)}) async-start(bf16[1,64,64,2,128]{4,2,3,0,1:T(8,128)(2,1)} %copy.44), calls=%async_computation.1 | async-start | bytes 4194304 | tf_op jit(solution)/shard_map/all_to_all | solution.py:85
  52.0 0.3 fusion.8
  52.3 2.0 %convolution_bitcast_fusion = f32[1,512,4,128]{3,1,2,0:T(8,128)S(1)} fusion(bf16[512,1024,1]{1,0,2:T(8,128)(2,1)S(1)} %bitcast.163, bf16[4,128,1024]{2,1,0:T(8,128)(2,1)} %bitcast.162), kind=kOutput, calls=%fused_computation.17 | convolution fusion | flops 536870912 | bytes 3145728 | tf_op jit(solution)/shard_map/dot_general | solution.py:77
  56.2 0.3 multiply_add_fusion.5
  57.0 0.3 multiply_add_fusion.4
  57.8 0.3 multiply_add_fusion.3
  58.5 0.3 multiply_add_fusion.2
  59.3 0.3 multiply_add_fusion.1
  60.1 0.3 multiply_add_fusion
  61.5 0.3 fusion.82
  61.8 86.7 %all-to-all-done.1 = bf16[1,64,64,2,128]{4,2,3,0,1:T(8,128)(2,1)S(1)} async-done(((bf16[1,64,64,2,128]{4,2,3,0,1:T(8,128)(2,1)}), bf16[1,64,64,2,128]{4,2,3,0,1:T(8,128)(2,1)S(1)}, u32[]{:S(2)}, u32[]{:S(2)}) %all-to-all-start.1) | async-done | bytes 2097184 | tf_op jit(solution)/shard_map/all_to_all | solution.py:85
  148.9 1.4 fusion
  150.5 2.2 %fusion.1 = f32[512]{0:T(512)S(1)} fusion(f32[512,4096]{1,0:T(8,128)S(1)} %get-tuple-element.44, f32[512]{0:T(512)S(1)} %maximum_maximum_fusion, pred[4096]{0:T(1024)(128)(4,1)S(1)} %lt.27), kind=kLoop, calls=%fused_computation.3 | loop fusion | flops 8388096 | bytes 8396800 | tf_op jit(solution)/shard_map/reduce_sum | solution.py:119
  152.7 1.7 fusion.3
  154.7 0.5 multiply_reduce_fusion
  155.6 0.5 broadcast.164
  156.1 1.4 reduce.5
  157.5 0.7 reshape.316
  158.2 8.6 %all-to-all-start.2 = ((bf16[8,2,4096]{2,1,0:T(2,128)(2,1)}), bf16[8,2,4096]{2,1,0:T(2,128)(2,1)S(1)}, u32[]{:S(2)}, u32[]{:S(2)}) async-start(bf16[8,2,4096]{2,1,0:T(2,128)(2,1)} %reshape.316), calls=%async_computation.2 | async-start | bytes 262144 | tf_op jit(solution)/shard_map/all_to_all | solution.py:159
  166.8 0.7 maximum_bitcast_fusion
  167.4 4.6 %all-to-all-done.2 = bf16[8,2,4096]{2,1,0:T(2,128)(2,1)S(1)} async-done(((bf16[8,2,4096]{2,1,0:T(2,128)(2,1)}), bf16[8,2,4096]{2,1,0:T(2,128)(2,1)S(1)}, u32[]{:S(2)}, u32[]{:S(2)}) %all-to-all-start.2) | async-done | bytes 131104 | tf_op jit(solution)/shard_map/all_to_all | solution.py:159
  172.2 2.0 %fusion.9 = bf16[1,64,8,1024]{3,1,2,0:T(8,128)(2,1)S(1)} fusion(bf16[64,8,128]{2,0,1:T(8,128)(2,1)S(1)} %bitcast.166, bf16[8,128,1024]{2,1,0:T(8,128)(2,1)} %bitcast.158), kind=kOutput, calls=%fused_computation.14 | convolution fusion | flops 134742016 | bytes 3276800 | tf_op jit(solution)/shard_map/atgc,gcd->atgd/dot_general | solution.py:166
  174.2 0.8 reduce_sum.94
  (62 shorter events, 7.2 us)
Async XLA Ops:
  9.2 28.4 %all-to-all-start = ((bf16[8,1,64,1024]{3,2,1,0:T(8,128)(2,1)}), bf16[8,1,64,1024]{3,2,1,0:T(8,128)(2,1)S(1)}, u32[]{:S(2)}, u32[]{:S(2)}) async-start(bf16[8,1,64,1024]{3,2,1,0:T(8,128)(2,1)} %stack.10), calls=%async_computation | async-start | bytes 2097152 | tf_op jit(solution)/shard_map/all_to_all | solution.py:70
  19.5 152.7 %all-gather.2.cloned.1.call-start = ((), (), s32[]{:S(2)}) async-start(), calls=%async_computation.3 | async-start | bytes 2359296 | tf_op jit(solution)/shard_map/all_gather | solution.py:161
  34.0 20.8 %copy-start.4 = (f32[2,1,1,128,128]{4,3,2,1,0:T(8,128)S(1)}, f32[2,1,1,128,128]{4,3,2,1,0:T(8,128)}, u32[]{:S(2)}) copy-start(f32[2,1,1,128,128]{4,3,2,1,0:T(8,128)} %param.23) | copy-start | bytes 393220
  37.5 23.4 %copy-start.5 = (bf16[2,16,128]{2,1,0:T(8,128)(2,1)S(1)}, bf16[2,16,128]{2,1,0:T(8,128)(2,1)}, u32[]{:S(2)}) copy-start(bf16[2,16,128]{2,1,0:T(8,128)(2,1)} %param.18) | copy-start | bytes 24580
  37.6 111.0 %all-to-all-start.1 = ((bf16[1,64,64,2,128]{4,2,3,0,1:T(8,128)(2,1)}), bf16[1,64,64,2,128]{4,2,3,0,1:T(8,128)(2,1)S(1)}, u32[]{:S(2)}, u32[]{:S(2)}) async-start(bf16[1,64,64,2,128]{4,2,3,0,1:T(8,128)(2,1)} %copy.44), calls=%async_computation.1 | async-start | bytes 4194304 | tf_op jit(solution)/shard_map/all_to_all | solution.py:85
  54.3 7.2 %copy-start = (f32[1,512,4,128]{3,1,2,0:T(8,128)}, f32[1,512,4,128]{3,1,2,0:T(8,128)S(1)}, u32[]{:S(2)}) copy-start(f32[1,512,4,128]{3,1,2,0:T(8,128)S(1)} %convolution_bitcast_fusion) | copy-start | bytes 3145732
  60.7 0.7 copy-start.2
  152.7 2.0 %copy-start.1 = (f32[1,512,4,128]{3,1,2,0:T(8,128)S(1)}, f32[1,512,4,128]{3,1,2,0:T(8,128)}, u32[]{:S(2)}) copy-start(f32[1,512,4,128]{3,1,2,0:T(8,128)} %copy-done) | copy-start | bytes 3145732
  152.7 2.5 %copy-start.3 = (f32[512,128]{1,0:T(8,128)S(1)}, f32[512,128]{1,0:T(8,128)}, u32[]{:S(2)}) copy-start(f32[512,128]{1,0:T(8,128)} %copy-done.2) | copy-start | bytes 786436
  158.2 13.9 %all-to-all-start.2 = ((bf16[8,2,4096]{2,1,0:T(2,128)(2,1)}), bf16[8,2,4096]{2,1,0:T(2,128)(2,1)S(1)}, u32[]{:S(2)}, u32[]{:S(2)}) async-start(bf16[8,2,4096]{2,1,0:T(2,128)(2,1)} %reshape.316), calls=%async_computation.2 | async-start | bytes 262144 | tf_op jit(solution)/shard_map/all_to_all | solution.py:159
Sparse Core Ops, SparseCore 0:
  22.4 33.2 all-gather.1
